TPU v7x, 32 devices: a whole 2x2x4 slice. The times are simulated.
32 devices in a mesh: groups: 2 (over y), rows: 4 (over z), zero: 4 (over x, core).
Axes of the slice: x: 2, y: 2, z: 4, core: 2. Of those that a mesh axis runs over, the one named last changes fastest.
Arguments:
- latents: bfloat16 [8, 320, 32, 128], P(('groups', 'zero'), None, 'rows'), parts along dimension 0, may hold values from -40 to 40
- time_shift: float32 [8, 320], P(('groups', 'zero')), parts along dimension 0, may hold values from -4 to 4
- conv_first: bfloat16 [320, 9, 320], P('zero'), may hold values from -0.109375 to 0.109375
- conv_second: bfloat16 [320, 9, 320], P('zero'), may hold values from -0.1875 to 0.1875
- norm_gains: float32 [2, 320], replicated, may hold values from 0.5 to 1.5
- norm_biases: float32 [2, 320], replicated, may hold values from -3 to 3
- grad_output: bfloat16 [8, 320, 32, 128], P(('groups', 'zero'), None, 'rows'), parts along dimension 0, may hold values from -40 to 40
Outputs:
- block_out: bfloat16 [8, 320, 32, 128], P(('groups', 'zero'), None, 'rows'), parts along dimension 0
- grad_input: bfloat16 [8, 320, 32, 128], P(('groups', 'zero'), None, 'rows'), parts along dimension 0
- grad_time: float32 [8, 320], P(('groups', 'zero')), parts along dimension 0
- grad_conv_first: float32 [640, 9, 320], P(('groups', 'zero')), parts along dimension 0
- grad_conv_second: float32 [640, 9, 320], P(('groups', 'zero')), parts along dimension 0
- grad_norms: float32 [8, 320], P('groups'), parts along dimension 0
There are 2 independent parts, one for each index of `groups`. A program takes and returns all parts, laid end to end along the dimension named above; an argument that names none is the same for every part. Nothing has to cross between parts.
All inputs are finite; a program needn't handle non-finite values.
Results may differ from a plain program's by a relative error of at most 0.0056.
Values may be sent and summed in bfloat16 or wider, within the bound.
A program may use at most 128 MiB of HBM per device.

v0:
```python
import jax
import jax.numpy as jnp
from jax import lax
from jax.sharding import PartitionSpec as P

NORM_GROUPS = 32
EPSILON = 1e-05


def with_halo(value, sides, width):
    for axis, dim in sides:
        devices, length = (lax.axis_size(axis), value.shape[dim])
        up = [(i, (i + 1) % devices) for i in range(devices - 1)]
        down = [(j, i) for i, j in up]
        last = lax.slice_in_dim(value, length - width, length, axis=dim)
        first = lax.slice_in_dim(value, 0, width, axis=dim)
        before = lax.ppermute(last, axis, up)
        after = lax.ppermute(first, axis, down)
        value = jnp.concatenate([before, value, after], axis=dim)
    return value


def shifted_stack(padded, flipped):
    height = padded.shape[2] - 2
    width = padded.shape[3]
    widened = jnp.pad(padded, ((0, 0), (0, 0), (0, 0), (1, 1)))
    slices = [
        widened[:, :, tap_row : tap_row + height, tap_col : tap_col + width]
        for tap_row in range(3)
        for tap_col in range(3)
    ]
    if flipped:
        slices = slices[::-1]
    return jnp.stack(slices, axis=1)


def with_faces(field):
    return with_halo(field, (("rows", 2),), 1)


def group_stats(values):
    images, channels, height, width = values.shape
    grouped = values.reshape(images, NORM_GROUPS, channels // NORM_GROUPS, height, width)
    members = channels // NORM_GROUPS * height * width * lax.axis_size("rows")
    totals, squares = lax.psum(
        (jnp.sum(grouped, axis=(2, 3, 4)), jnp.sum(grouped * grouped, axis=(2, 3, 4))), "rows"
    )
    average = totals / members
    centered = grouped - average[:, :, None, None, None]
    variance = squares / members - average * average
    scaling = lax.rsqrt(variance + EPSILON)
    return ((centered * scaling[:, :, None, None, None]).reshape(values.shape), scaling)


def norm_backward(grad_normed, normed, scaling):
    images, channels, height, width = normed.shape
    shape = (images, NORM_GROUPS, channels // NORM_GROUPS, height, width)
    members = channels // NORM_GROUPS * height * width * lax.axis_size("rows")
    grouped_grad = grad_normed.reshape(shape)
    grouped_norm = normed.reshape(shape)
    group_sum, cross_sum = lax.psum(
        (
            jnp.sum(grouped_grad, axis=(2, 3, 4)),
            jnp.sum(grouped_grad * grouped_norm, axis=(2, 3, 4)),
        ),
        "rows",
    )
    result = scaling[:, :, None, None, None] * (
        grouped_grad
        - (group_sum / members)[:, :, None, None, None]
        - grouped_norm * (cross_sum / members)[:, :, None, None, None]
    )
    return result.reshape(normed.shape)


def silu_slope(pre_values):
    logistic = jax.nn.sigmoid(pre_values)
    return logistic * (1.0 + pre_values * (1.0 - logistic))


def forward_conv(stacked, shard):
    return jnp.einsum(
        "otc,ntchw->nohw",
        lax.all_gather(shard, "zero", axis=0, tiled=True),
        stacked,
        preferred_element_type=jnp.float32,
    )


def backward_conv(stacked_grad, shard):
    return jnp.einsum(
        "otc,ntohw->nchw",
        lax.all_gather(shard, "zero", axis=0, tiled=True),
        stacked_grad,
        preferred_element_type=jnp.float32,
    )


def weight_gradient(cotangent, stacked):
    share = lax.psum_scatter(
        jnp.einsum("nohw,ntchw->otc", cotangent, stacked, preferred_element_type=jnp.float32),
        "zero",
        scatter_dimension=0,
        tiled=True,
    )
    return lax.psum(share, "rows")


def local(latents, time_shift, conv_first, conv_second, norm_gains, norm_biases, grad_output):
    gain_first = norm_gains[0][None, :, None, None]
    gain_second = norm_gains[1][None, :, None, None]
    bias_first = norm_biases[0][None, :, None, None]
    bias_second = norm_biases[1][None, :, None, None]
    normed_first, scale_first = group_stats(latents.astype(jnp.float32))
    pre_first = gain_first * normed_first + bias_first
    act_first = jax.nn.silu(pre_first).astype(jnp.bfloat16)
    stack_first = shifted_stack(with_faces(act_first), False)
    conv_out = forward_conv(stack_first, conv_first)
    hidden = (conv_out + time_shift[:, :, None, None]).astype(jnp.bfloat16)
    normed_second, scale_second = group_stats(hidden.astype(jnp.float32))
    pre_second = gain_second * normed_second + bias_second
    act_second = jax.nn.silu(pre_second).astype(jnp.bfloat16)
    stack_second = shifted_stack(with_faces(act_second), False)
    second_out = forward_conv(stack_second, conv_second)
    block_out = (latents.astype(jnp.float32) + second_out).astype(jnp.bfloat16)
    grad_conv_second = weight_gradient(grad_output, stack_second)
    stack_grad = shifted_stack(with_faces(grad_output), True)
    back_second = backward_conv(stack_grad, conv_second)
    slope_second = back_second * silu_slope(pre_second)
    grad_hidden = norm_backward(gain_second * slope_second, normed_second, scale_second)
    grad_time = lax.psum(jnp.sum(grad_hidden, axis=(2, 3)), "rows")
    hidden_grad = grad_hidden.astype(jnp.bfloat16)
    grad_conv_first = weight_gradient(hidden_grad, stack_first)
    stack_hidden = shifted_stack(with_faces(hidden_grad), True)
    back_first = backward_conv(stack_hidden, conv_first)
    slope_first = back_first * silu_slope(pre_first)
    grad_latent = norm_backward(gain_first * slope_first, normed_first, scale_first)
    grad_input = (grad_output.astype(jnp.float32) + grad_latent).astype(jnp.bfloat16)
    local_terms = jnp.stack(
        [
            jnp.sum(slope_first * normed_first, axis=(0, 2, 3)),
            jnp.sum(slope_first, axis=(0, 2, 3)),
            jnp.sum(slope_second * normed_second, axis=(0, 2, 3)),
            jnp.sum(slope_second, axis=(0, 2, 3)),
        ]
    )
    grad_norms = lax.psum(local_terms, ("rows", "zero"))
    return (block_out, grad_input, grad_time, grad_conv_first, grad_conv_second, grad_norms)


def solution(mesh):
    placed = (
        P(("groups", "zero"), None, "rows", None),
        P(("groups", "zero"), None),
        P("zero", None, None),
        P("zero", None, None),
        P(),
        P(),
        P(("groups", "zero"), None, "rows", None),
    )
    return jax.shard_map(
        local,
        mesh=mesh,
        in_specs=placed,
        out_specs=(
            P(("groups", "zero"), None, "rows", None),
            P(("groups", "zero"), None, "rows", None),
            P(("groups", "zero"), None),
            P(("groups", "zero"), None, None),
            P(("groups", "zero"), None, None),
            P("groups", None),
        ),
        check_vma=False,
    )
```

profile of v0, /device:TPU:0, one launch (start us, length us, event | category | flops | bytes accessed | tf_op | source)
XLA Modules:
  0.0 314.7 jit_solution(3994753162945767644)
XLA Ops:
  9.8 13.5 %all-reduce.7 = (f32[1,32]{1,0:T(1,128)S(1)}, f32[1,32]{1,0:T(1,128)S(1)}) all-reduce(f32[1,32]{1,0:T(1,128)S(1)} %bitcast.372, f32[1,32]{1,0:T(1,128)S(1)} %bitcast.371), channel_id=1, replica_groups=mesh['groups'=2,'rows'=4,'zero'=4] {'rows'}, use_global_device_ids=true, to_apply=%region_5.6 | all-reduce | flops 64 | bytes 512 | tf_op jit(solution)/shard_map/psum | solution.py:45
  27.9 4.6 %collective-permute-start.4 = (bf16[1,320,1,128]{3,1,2,0:T(8,128)(2,1)S(1)}, bf16[1,320,1,128]{3,1,2,0:T(8,128)(2,1)S(1)}, u32[]{:S(2)}, u32[]{:S(2)}) collective-permute-start(bf16[1,320,1,128]{3,1,2,0:T(8,128)(2,1)S(1)} %get-tuple-element.56), channel_id=1, source_target_pairs={{0,4},{4,8},{8,12},{1,5},{5,9},{9,13},{2,6},{6,10},{10,14},{3,7},{... | collective-permute-start | bytes 245768 | tf_op jit(solution)/shard_map/ppermute | solution.py:17
  36.7 2.0 collective-permute-done.5
  48.3 2.6 copy-done.4
  51.8 5.8 %convert_reduce_fusion.1 = (f32[320]{0:T(512)S(1)}, f32[320]{0:T(512)S(1)}, bf16[1,8,128,320]{2,3,1,0:T(8,128)(2,1)S(1)}) fusion(f32[320]{0:T(512)S(1)} %reduce.34, bf16[1,9,320,8,128]{4,2,1,3,0:T(8,128)(2,1)} %copy-done.4, bf16[320,9,320]{2,0,1:T(8,128)(2,1)} %all-gather.3.cloned.1.call-done), kind=kOutput, calls=%fused_computation.26 | convolution fusion | flops 1889402368 | bytes 8400640 | tf_op jit(solution)/shard_map/otc,ntchw->nohw/dot_general | solution.py:82
  58.0 9.6 %all-reduce.6 = (f32[1,32]{1,0:T(1,128)S(1)}, f32[1,32]{1,0:T(1,128)S(1)}) all-reduce(f32[1,32]{1,0:T(1,128)S(1)} %bitcast.373, f32[1,32]{1,0:T(1,128)S(1)} %bitcast.369), channel_id=1, replica_groups=mesh['groups'=2,'rows'=4,'zero'=4] {'rows'}, use_global_device_ids=true, to_apply=%region_11.12 | all-reduce | flops 64 | bytes 512 | tf_op jit(solution)/shard_map/psum | solution.py:45
  68.0 6.4 %fusion.83 = (f32[320]{0:T(512)S(1)}, f32[320]{0:T(512)S(1)}, f32[320]{0:T(512)S(1)}, f32[320]{0:T(512)S(1)}, f32[1,320,8,128]{3,1,2,0:T(8,128)S(1)}) fusion(bf16[1,8,128,320]{2,3,1,0:T(8,128)(2,1)S(1)} %get-tuple-element.66, f32[320]{0:T(512)S(1)} %mul.235, f32[320]{0:T(512)S(1)} %sub.127, f32[320]{0:T(512)S(1)} %get-tuple-element.70, ...), kind=kOutput, calls=%fused_computation.64 | convolution fusion | flops 1893989376 | bytes 9717760 | tf_op jit(solution)/shard_map/otc,ntohw->nchw/dot_general | solution.py:91
  74.8 9.4 %all-reduce.5 = (f32[1,32]{1,0:T(1,128)S(1)}, f32[1,32]{1,0:T(1,128)S(1)}) all-reduce(f32[1,32]{1,0:T(1,128)S(1)} %bitcast.374, f32[1,32]{1,0:T(1,128)S(1)} %bitcast.370), channel_id=1, replica_groups=mesh['groups'=2,'rows'=4,'zero'=4] {'rows'}, use_global_device_ids=true, to_apply=%region_17.18 | all-reduce | flops 64 | bytes 512 | tf_op jit(solution)/shard_map/psum | solution.py:61
  84.6 2.1 fusion.154
  86.7 2.9 collective-permute-start.2
  91.6 4.3 %collective-permute-done.3 = bf16[1,320,1,128]{3,1,2,0:T(8,128)(2,1)S(1)} collective-permute-done((bf16[1,320,1,128]{3,1,2,0:T(8,128)(2,1)S(1)}, bf16[1,320,1,128]{3,1,2,0:T(8,128)(2,1)S(1)}, u32[]{:S(2)}, u32[]{:S(2)}) %collective-permute-start.3) | collective-permute-done | bytes 81952 | tf_op jit(solution)/shard_map/ppermute | solution.py:18
  98.6 4.8 %fusion.4 = f32[9,320,320,1]{2,1,3,0:T(8,128)} fusion(bf16[1,9,320,8,128]{4,2,3,1,0:T(8,128)(2,1)S(1)} %fusion.131, bf16[320,8,128]{2,1,0:T(8,128)(2,1)S(1)} %bitcast.365), kind=kOutput, calls=%fused_computation.4 | convolution fusion | flops 1887436800 | bytes 10240000 | tf_op jit(solution)/shard_map/nohw,ntchw->otc/dot_general | solution.py:101
  103.5 5.6 %copy.103 = f32[320,2880]{1,0:T(8,128)} copy(f32[320,2880]{0,1:T(8,128)} %bitcast.366) | data formatting | bytes 7372800
  109.1 8.1 %fusion.17 = f32[320,9,320]{2,0,1:T(8,128)} fusion(bf16[1,9,320,8,128]{4,2,1,3,0:T(8,128)(2,1)} %copy-done.4, bf16[1,320,8,128]{3,1,2,0:T(8,128)(2,1)S(1)} %get-tuple-element.52), kind=kOutput, calls=%fused_computation.23 | convolution fusion | flops 1887436800 | bytes 10240000 | tf_op jit(solution)/shard_map/nohw,ntchw->otc/dot_general | solution.py:101
  121.3 4.3 %collective-permute-done.7 = bf16[1,320,1,128]{3,1,2,0:T(8,128)(2,1)S(1)} collective-permute-done((bf16[1,320,1,128]{3,1,2,0:T(8,128)(2,1)S(1)}, bf16[1,320,1,128]{3,1,2,0:T(8,128)(2,1)S(1)}, u32[]{:S(2)}, u32[]{:S(2)}) %collective-permute-start.7) | collective-permute-done | bytes 81952 | tf_op jit(solution)/shard_map/ppermute | solution.py:18
  135.4 14.0 %reduce-scatter.7.cloned.1.call-done = f32[80,2880]{1,0:T(8,128)} async-done(((f32[320,2880]{1,0:T(8,128)}), f32[80,2880]{1,0:T(8,128)}) %reduce-scatter.7.cloned.1.call-update) | async-done | bytes 921616
  149.4 2.8 copy.104
  152.1 45.8 %reduce-scatter.5.cloned.1.call-done = f32[80,9,320]{2,0,1:T(8,128)} async-done(((f32[320,9,320]{2,0,1:T(8,128)}), f32[80,9,320]{2,0,1:T(8,128)}) %reduce-scatter.5.cloned.1.call-update) | async-done | bytes 921616 | tf_op jit(solution)/shard_map/reduce_scatter | solution.py:100
  198.0 6.4 %fusion.105 = (f32[320]{0:T(512)S(1)}, f32[320]{0:T(512)S(1)}, f32[320]{0:T(512)S(1)}, f32[320]{0:T(512)S(1)}, f32[1,320,8,128]{3,1,2,0:T(8,128)S(1)}) fusion(f32[320]{0:T(512)S(1)} %mul.226, f32[320]{0:T(512)S(1)} %sub.121, bf16[1,320,8,128]{3,2,1,0:T(8,128)(2,1)S(1)} %copy-done, f32[320]{0:T(512)S(1)} %get-tuple-element.69, ...), kind=kOutput, calls=%fused_computation.86 | convolution fusion | flops 1893989376 | bytes 9717760 | tf_op jit(solution)/shard_map/otc,ntohw->nchw/dot_general | solution.py:91
  204.8 12.6 %all-reduce.4 = (f32[1,32]{1,0:T(1,128)S(1)}, f32[1,32]{1,0:T(1,128)S(1)}, f32[1,320]{1,0:T(1,128)}) all-reduce(f32[1,32]{1,0:T(1,128)S(1)} %bitcast.368, f32[1,32]{1,0:T(1,128)S(1)} %bitcast.367, f32[1,320]{1,0:T(1,128)S(1)} %reduce_sum.224), channel_id=1, replica_groups=mesh['groups'=2,'rows'=4,'zero'=4] {'rows'}, use_global_device_ids=true, to_apply=%region_23.24 | all-reduce | flops 384 | bytes 3072 | tf_op jit(solution)/shard_map/psum | solution.py:61
  219.7 5.0 %fusion.59 = bf16[1,320,8,128]{3,1,2,0:T(8,128)(2,1)S(1)} fusion(bf16[1,9,320,8,128]{4,2,3,1,0:T(8,128)(2,1)} %copy-done.5, bf16[320,9,320]{2,0,1:T(8,128)(2,1)S(1)} %copy-done.7, bf16[1,320,8,128]{3,2,1,0:T(8,128)(2,1)S(1)} %copy-done), kind=kOutput, calls=%fused_computation.44 | convolution fusion | flops 1888419840 | bytes 9052160 | tf_op jit(solution)/shard_map/otc,ntchw->nohw/dot_general | solution.py:82
  225.9 33.0 %psum.95 = f32[4,320]{1,0:T(4,128)} all-reduce(f32[4,320]{1,0:T(4,128)S(1)} %pad_maximum_fusion.8), channel_id=1, replica_groups=mesh['groups'=2,'rows'=4,'zero'=4] {'rows','zero'}, use_global_device_ids=true, to_apply=%region_34.35 | all-reduce | flops 1280 | bytes 10240 | tf_op jit(solution)/shard_map/psum | solution.py:147
  259.0 45.2 %all-reduce.11.cloned.1.call-done = (f32[80,9,320]{2,0,1:T(8,128)}, f32[80,9,320]{0,2,1:T(8,128)}) async-done(((f32[80,9,320]{2,0,1:T(8,128)}, f32[80,9,320]{0,2,1:T(8,128)}), (f32[80,9,320]{2,0,1:T(8,128)}, f32[80,9,320]{0,2,1:T(8,128)})) %all-reduce.11.cloned.1.call-update) | async-done | bytes 1843216 | tf_op jit(solution)/shard_map/psum | solution.py:106
  304.2 3.0 copy.94
  (135 shorter events, 46.9 us)
Async XLA Ops:
  7.2 17.3 %copy-start = (bf16[1,320,8,128]{3,2,1,0:T(8,128)(2,1)S(1)}, bf16[1,320,8,128]{3,2,1,0:T(8,128)(2,1)}, u32[]{:S(2)}) copy-start(bf16[1,320,8,128]{3,2,1,0:T(8,128)(2,1)} %param.7) | copy-start | bytes 1966084
  7.2 20.6 %copy-start.1 = (bf16[1,320,8,128]{3,2,1,0:T(8,128)(2,1)S(1)}, bf16[1,320,8,128]{3,2,1,0:T(8,128)(2,1)}, u32[]{:S(2)}) copy-start(bf16[1,320,8,128]{3,2,1,0:T(8,128)(2,1)} %param.13) | copy-start | bytes 1966084
  7.2 44.6 %all-gather.3.cloned.1.call-start = ((), (), s32[]{:S(2)}) async-start(), calls=%async_computation.2 | async-start | bytes 2764800 | tf_op jit(solution)/shard_map/all_gather | solution.py:84
  7.9 60.1 %all-gather.5.cloned.1.call-start = ((), (), s32[]{:S(2)}) async-start(), calls=%async_computation.3 | async-start | bytes 2764800 | tf_op jit(solution)/shard_map/all_gather | solution.py:84
  24.4 9.3 %copy-start.6 = (f32[1,320]{1,0:T(1,128)S(1)}, f32[1,320]{1,0:T(1,128)}, u32[]{:S(2)}) copy-start(f32[1,320]{1,0:T(1,128)} %param.8) | copy-start | bytes 3844
  25.1 8.7 %collective-permute-start = (bf16[1,320,1,128]{3,1,2,0:T(8,128)(2,1)S(1)}, bf16[1,320,1,128]{3,1,2,0:T(8,128)(2,1)S(1)}, u32[]{:S(2)}, u32[]{:S(2)}) collective-permute-start(bf16[1,320,1,128]{3,1,2,0:T(8,128)(2,1)S(1)} %get-tuple-element.60), channel_id=1, source_target_pairs={{0,4},{4,8},{8,12},{1,5},{5,9},{9,13},{2,6},{6,10},{10,14},{3,7},{... | collective-permute-start | bytes 245768 | tf_op jit(solution)/shard_map/ppermute | solution.py:17
  26.4 7.4 %collective-permute-start.1 = (bf16[1,320,1,128]{3,1,2,0:T(8,128)(2,1)S(1)}, bf16[1,320,1,128]{3,1,2,0:T(8,128)(2,1)S(1)}, u32[]{:S(2)}, u32[]{:S(2)}) collective-permute-start(bf16[1,320,1,128]{3,1,2,0:T(8,128)(2,1)S(1)} %get-tuple-element.61), channel_id=1, source_target_pairs={{4,0},{8,4},{12,8},{5,1},{9,5},{13,9},{6,2},{10,6},{14,10},{7,3},{... | collective-permute-start | bytes 245768 | tf_op jit(solution)/shard_map/ppermute | solution.py:18
  27.9 8.9 %collective-permute-start.4 = (bf16[1,320,1,128]{3,1,2,0:T(8,128)(2,1)S(1)}, bf16[1,320,1,128]{3,1,2,0:T(8,128)(2,1)S(1)}, u32[]{:S(2)}, u32[]{:S(2)}) collective-permute-start(bf16[1,320,1,128]{3,1,2,0:T(8,128)(2,1)S(1)} %get-tuple-element.56), channel_id=1, source_target_pairs={{0,4},{4,8},{8,12},{1,5},{5,9},{9,13},{2,6},{6,10},{10,14},{3,7},{... | collective-permute-start | bytes 245768 | tf_op jit(solution)/shard_map/ppermute | solution.py:17
  32.4 6.3 %collective-permute-start.5 = (bf16[1,320,1,128]{3,1,2,0:T(8,128)(2,1)S(1)}, bf16[1,320,1,128]{3,1,2,0:T(8,128)(2,1)S(1)}, u32[]{:S(2)}, u32[]{:S(2)}) collective-permute-start(bf16[1,320,1,128]{3,1,2,0:T(8,128)(2,1)S(1)} %get-tuple-element.57), channel_id=1, source_target_pairs={{4,0},{8,4},{12,8},{5,1},{9,5},{13,9},{6,2},{10,6},{14,10},{7,3},{... | collective-permute-start | bytes 245768 | tf_op jit(solution)/shard_map/ppermute | solution.py:18
  33.7 115.6 %reduce-scatter.7.cloned.1.call-start = ((), (), s32[]{:S(2)}) async-start(), calls=%async_computation.5 | async-start | bytes 4710400
  48.2 2.6 copy-start.4
  57.6 16.8 %copy-start.3 = (bf16[1,8,128,320]{2,3,1,0:T(8,128)(2,1)}, bf16[1,8,128,320]{2,3,1,0:T(8,128)(2,1)S(1)}, u32[]{:S(2)}) copy-start(bf16[1,8,128,320]{2,3,1,0:T(8,128)(2,1)S(1)} %get-tuple-element.66) | copy-start | bytes 1966084
  86.7 5.0 %collective-permute-start.2 = (bf16[1,320,1,128]{3,1,2,0:T(8,128)(2,1)S(1)}, bf16[1,320,1,128]{3,1,2,0:T(8,128)(2,1)S(1)}, u32[]{:S(2)}, u32[]{:S(2)}) collective-permute-start(bf16[1,320,1,128]{3,1,2,0:T(8,128)(2,1)S(1)} %get-tuple-element.58), channel_id=1, source_target_pairs={{0,4},{4,8},{8,12},{1,5},{5,9},{9,13},{2,6},{6,10},{10,14},{3,7},{... | collective-permute-start | bytes 245768 | tf_op jit(solution)/shard_map/ppermute | solution.py:17
  89.6 6.3 %collective-permute-start.3 = (bf16[1,320,1,128]{3,1,2,0:T(8,128)(2,1)S(1)}, bf16[1,320,1,128]{3,1,2,0:T(8,128)(2,1)S(1)}, u32[]{:S(2)}, u32[]{:S(2)}) collective-permute-start(bf16[1,320,1,128]{3,1,2,0:T(8,128)(2,1)S(1)} %get-tuple-element.59), channel_id=1, source_target_pairs={{4,0},{8,4},{12,8},{5,1},{9,5},{13,9},{6,2},{10,6},{14,10},{7,3},{... | collective-permute-start | bytes 245768 | tf_op jit(solution)/shard_map/ppermute | solution.py:18
  98.6 4.9 %copy-start.5 = (bf16[1,9,320,8,128]{4,2,3,1,0:T(8,128)(2,1)}, bf16[1,9,320,8,128]{4,2,3,1,0:T(8,128)(2,1)S(1)}, u32[]{:S(2)}) copy-start(bf16[1,9,320,8,128]{4,2,3,1,0:T(8,128)(2,1)S(1)} %fusion.131) | copy-start | bytes 17694724
  109.1 88.9 %reduce-scatter.5.cloned.1.call-start = ((), (), s32[]{:S(2)}) async-start(), calls=%async_computation.4 | async-start | bytes 5529600 | tf_op jit(solution)/shard_map/reduce_scatter | solution.py:100
  117.3 186.9 %all-reduce.11.cloned.1.call-start = ((), (), s32[]{:S(2)}) async-start(), calls=%async_computation.6 | async-start | bytes 5160960 | tf_op jit(solution)/shard_map/psum | solution.py:106
  117.3 4.0 %collective-permute-start.6 = (bf16[1,320,1,128]{3,1,2,0:T(8,128)(2,1)S(1)}, bf16[1,320,1,128]{3,1,2,0:T(8,128)(2,1)S(1)}, u32[]{:S(2)}, u32[]{:S(2)}) collective-permute-start(bf16[1,320,1,128]{3,1,2,0:T(8,128)(2,1)S(1)} %get-tuple-element.54), channel_id=1, source_target_pairs={{0,4},{4,8},{8,12},{1,5},{5,9},{9,13},{2,6},{6,10},{10,14},{3,7},{... | collective-permute-start | bytes 245768 | tf_op jit(solution)/shard_map/ppermute | solution.py:17
  119.3 6.3 %collective-permute-start.7 = (bf16[1,320,1,128]{3,1,2,0:T(8,128)(2,1)S(1)}, bf16[1,320,1,128]{3,1,2,0:T(8,128)(2,1)S(1)}, u32[]{:S(2)}, u32[]{:S(2)}) collective-permute-start(bf16[1,320,1,128]{3,1,2,0:T(8,128)(2,1)S(1)} %get-tuple-element.55), channel_id=1, source_target_pairs={{4,0},{8,4},{12,8},{5,1},{9,5},{13,9},{6,2},{10,6},{14,10},{7,3},{... | collective-permute-start | bytes 245768 | tf_op jit(solution)/shard_map/ppermute | solution.py:18
  217.8 1.9 copy-start.7
  304.2 3.0 copy-start.2
Sparse Core Ops, SparseCore 0:
  9.6 25.9 all-gather.2
  37.1 23.2 all-gather.4
  109.2 40.1 reduce-scatter.6
  152.0 45.9 reduce-scatter.4
  200.3 103.8 all-reduce.10
where the time goes:
time: 315 us
  waiting for transfers between devices  118 us (37%)
  blocking collectives  78 us (25%)
  local copies, waits for them, and re-layouts  38.1 us (12%)
  matrix products  36.4 us (12%)
  starting transfers between devices  16.3 us (5%)
  between operations  14.3 us (5%)
  other arithmetic  14 us (4%)
    reduce_scatter x1, waiting for transfers between devices, weight_gradient(): lax.psum_scatter(jnp.einsum('nohw,ntchw->otc', cotangent, stacked, prefer...  45.8 us
    psum x1, waiting for transfers between devices, weight_gradient(): return lax.psum(share, 'rows')  45.2 us
    psum x1, blocking collectives, local(): grad_norms = lax.psum(local_terms, ('rows', 'zero'))  33 us
    unnamed x46, local copies, waits for them, and re-layouts  32.3 us
    psum x2, blocking collectives, group_stats(): lax.psum((jnp.sum(grouped, axis=(2, 3, 4)), jnp.sum(grouped * grouped, ax...  23 us
    psum x2, blocking collectives, norm_backward(): lax.psum((jnp.sum(grouped_grad, axis=(2, 3, 4)), jnp.sum(grouped_grad * g...  22 us
    unnamed x6, waiting for transfers between devices  14.7 us
    dot_general x2, matrix products, weight_gradient(): jnp.einsum('nohw,ntchw->otc', cotangent, stacked, preferred_element_type=...  12.9 us
  transfers between devices with their start and end apart: 13, of which 8 were waited for; matrix products, arithmetic and copies ran while one was open for 19% of the time, Pallas kernels for 0%

commit v1 on v0

--- a/solution.py
+++ b/solution.py
@@ -103,7 +103,7 @@
         scatter_dimension=0,
         tiled=True,
     )
-    return lax.psum(share, "rows")
+    return jnp.sum(lax.all_gather(share, "rows"), axis=0)
 
 
 def local(latents, time_shift, conv_first, conv_second, norm_gains, norm_biases, grad_output):

time: 315 us -> 368 us (1.17)
  waiting for transfers between devices: 118 us -> 175 us
  local copies, waits for them, and re-layouts: 38.1 us -> 30.6 us
  other arithmetic: 14 us -> 20 us
    all_gather x0 -> x2, waiting for transfers between devices: none -> 95.6 us  [weight_gradient(): return jnp.sum(lax.all_gather(share, 'rows'), axis=0)]
    psum x1 -> x0, waiting for transfers between devices: 45.2 us -> none  [weight_gradient(): return lax.psum(share, 'rows')]
    unnamed x6 -> x7, waiting for transfers between devices: 14.7 us -> 45.2 us
    reduce_scatter x1, waiting for transfers between devices: 45.8 us -> 21.8 us  [weight_gradient(): lax.psum_scatter(jnp.einsum('nohw,ntchw->otc', cotangent, stacked, prefer...]
    unnamed x46 -> x44, local copies, waits for them, and re-layouts: 32.3 us -> 24.2 us
    reduce_sum x0 -> x2, other arithmetic: none -> 7.25 us  [weight_gradient(): return jnp.sum(lax.all_gather(share, 'rows'), axis=0)]
  transfers between devices with their start and end apart: 13 -> 14, of which waited for: 8 -> 9; matrix products, arithmetic and copies ran while one was open for 19% -> 16% of each run, Pallas kernels for 0% -> 0%
where the time goes in v1:
time: 368 us
  waiting for transfers between devices  175 us (48%)
  blocking collectives  75.2 us (20%)
  matrix products  33.9 us (9%)
  local copies, waits for them, and re-layouts  30.6 us (8%)
  other arithmetic  20 us (5%)
  starting transfers between devices  17.8 us (5%)
  between operations  14.7 us (4%)
    all_gather x2, waiting for transfers between devices, weight_gradient(): return jnp.sum(lax.all_gather(share, 'rows'), axis=0)  95.6 us
    unnamed x7, waiting for transfers between devices  45.2 us
    psum x1, blocking collectives, local(): grad_norms = lax.psum(local_terms, ('rows', 'zero'))  32.3 us
    unnamed x44, local copies, waits for them, and re-layouts  24.2 us
    psum x2, blocking collectives, group_stats(): lax.psum((jnp.sum(grouped, axis=(2, 3, 4)), jnp.sum(grouped * grouped, ax...  23 us
    reduce_scatter x1, waiting for transfers between devices, weight_gradient(): lax.psum_scatter(jnp.einsum('nohw,ntchw->otc', cotangent, stacked, prefer...  21.8 us
    psum x2, blocking collectives, norm_backward(): lax.psum((jnp.sum(grouped_grad, axis=(2, 3, 4)), jnp.sum(grouped_grad * g...  19.9 us
    dot_general x2, matrix products, weight_gradient(): jnp.einsum('nohw,ntchw->otc', cotangent, stacked, preferred_element_type=...  13 us
  transfers between devices with their start and end apart: 14, of which 9 were waited for; matrix products, arithmetic and copies ran while one was open for 16% of the time, Pallas kernels for 0%

profile of v1, /device:TPU:0, one launch (start us, length us, event | category | flops | bytes accessed | tf_op | source)
XLA Modules:
  0.0 367.6 jit_solution(17380237841301513601)
XLA Ops:
  9.8 13.5 %all-reduce.7 = (f32[1,32]{1,0:T(1,128)S(1)}, f32[1,32]{1,0:T(1,128)S(1)}) all-reduce(f32[1,32]{1,0:T(1,128)S(1)} %bitcast.376, f32[1,32]{1,0:T(1,128)S(1)} %bitcast.375), channel_id=1, replica_groups=mesh['groups'=2,'rows'=4,'zero'=4] {'rows'}, use_global_device_ids=true, to_apply=%region_5.6 | all-reduce | flops 64 | bytes 512 | tf_op jit(solution)/shard_map/psum | solution.py:45
  27.8 4.6 %collective-permute-start.4 = (bf16[1,320,1,128]{3,1,2,0:T(8,128)(2,1)S(1)}, bf16[1,320,1,128]{3,1,2,0:T(8,128)(2,1)S(1)}, u32[]{:S(2)}, u32[]{:S(2)}) collective-permute-start(bf16[1,320,1,128]{3,1,2,0:T(8,128)(2,1)S(1)} %get-tuple-element.54), channel_id=1, source_target_pairs={{0,4},{4,8},{8,12},{1,5},{5,9},{9,13},{2,6},{6,10},{10,14},{3,7},{... | collective-permute-start | bytes 245768 | tf_op jit(solution)/shard_map/ppermute | solution.py:17
  48.3 2.5 copy-done.3
  51.8 5.8 %convert_reduce_fusion.1 = (f32[320]{0:T(512)S(1)}, f32[320]{0:T(512)S(1)}, bf16[1,8,128,320]{2,3,1,0:T(8,128)(2,1)S(1)}) fusion(f32[320]{0:T(512)S(1)} %reduce.34, bf16[1,9,320,8,128]{4,2,1,3,0:T(8,128)(2,1)} %copy-done.3, bf16[320,9,320]{2,0,1:T(8,128)(2,1)} %all-gather.7.cloned.1.call-done), kind=kOutput, calls=%fused_computation.26 | convolution fusion | flops 1889402368 | bytes 8400640 | tf_op jit(solution)/shard_map/otc,ntchw->nohw/dot_general | solution.py:82
  58.0 9.6 %all-reduce.6 = (f32[1,32]{1,0:T(1,128)S(1)}, f32[1,32]{1,0:T(1,128)S(1)}) all-reduce(f32[1,32]{1,0:T(1,128)S(1)} %bitcast.377, f32[1,32]{1,0:T(1,128)S(1)} %bitcast.373), channel_id=1, replica_groups=mesh['groups'=2,'rows'=4,'zero'=4] {'rows'}, use_global_device_ids=true, to_apply=%region_11.12 | all-reduce | flops 64 | bytes 512 | tf_op jit(solution)/shard_map/psum | solution.py:45
  68.0 7.3 %fusion.83 = (f32[320]{0:T(512)S(1)}, f32[320]{0:T(512)S(1)}, f32[320]{0:T(512)S(1)}, f32[320]{0:T(512)S(1)}, f32[1,320,8,128]{3,1,2,0:T(8,128)}) fusion(bf16[1,8,128,320]{2,3,1,0:T(8,128)(2,1)S(1)} %get-tuple-element.64, f32[320]{0:T(512)S(1)} %mul.235, f32[320]{0:T(512)S(1)} %sub.127, f32[320]{0:T(512)S(1)} %get-tuple-element.68, ...), kind=kOutput, calls=%fused_computation.64 | convolution fusion | flops 1893989376 | bytes 9717760 | tf_op jit(solution)/shard_map/otc,ntohw->nchw/dot_general | solution.py:91
  75.7 9.4 %all-reduce.5 = (f32[1,32]{1,0:T(1,128)S(1)}, f32[1,32]{1,0:T(1,128)S(1)}) all-reduce(f32[1,32]{1,0:T(1,128)S(1)} %bitcast.378, f32[1,32]{1,0:T(1,128)S(1)} %bitcast.374), channel_id=1, replica_groups=mesh['groups'=2,'rows'=4,'zero'=4] {'rows'}, use_global_device_ids=true, to_apply=%region_17.18 | all-reduce | flops 64 | bytes 512 | tf_op jit(solution)/shard_map/psum | solution.py:61
  87.7 8.1 %fusion.17 = f32[320,9,320]{2,0,1:T(8,128)} fusion(bf16[1,9,320,8,128]{4,2,1,3,0:T(8,128)(2,1)} %copy-done.3, bf16[1,320,8,128]{3,1,2,0:T(8,128)(2,1)S(1)} %get-tuple-element.50), kind=kOutput, calls=%fused_computation.23 | convolution fusion | flops 1887436800 | bytes 10240000 | tf_op jit(solution)/shard_map/nohw,ntchw->otc/dot_general | solution.py:101
  95.9 2.9 collective-permute-start.2
  100.9 4.3 %collective-permute-done.3 = bf16[1,320,1,128]{3,1,2,0:T(8,128)(2,1)S(1)} collective-permute-done((bf16[1,320,1,128]{3,1,2,0:T(8,128)(2,1)S(1)}, bf16[1,320,1,128]{3,1,2,0:T(8,128)(2,1)S(1)}, u32[]{:S(2)}, u32[]{:S(2)}) %collective-permute-start.3) | collective-permute-done | bytes 81952 | tf_op jit(solution)/shard_map/ppermute | solution.py:18
  107.9 4.9 %fusion.4 = f32[9,320,320,1]{2,1,3,0:T(8,128)} fusion(bf16[1,9,320,8,128]{4,2,3,1,0:T(8,128)(2,1)S(1)} %fusion.131, bf16[320,8,128]{2,1,0:T(8,128)(2,1)S(1)} %bitcast.367), kind=kOutput, calls=%fused_computation.4 | convolution fusion | flops 1887436800 | bytes 10240000 | tf_op jit(solution)/shard_map/nohw,ntchw->otc/dot_general | solution.py:101
  112.7 6.1 %copy.102 = f32[320,2880]{1,0:T(8,128)} copy(f32[320,2880]{0,1:T(8,128)} %bitcast.370) | data formatting | bytes 7372800
  118.9 21.8 %reduce-scatter.5.cloned.1.call-done = f32[80,9,320]{2,0,1:T(8,128)} async-done(((f32[320,9,320]{2,0,1:T(8,128)}), f32[80,9,320]{2,0,1:T(8,128)}) %reduce-scatter.5.cloned.1.call-update) | async-done | bytes 921616 | tf_op jit(solution)/shard_map/reduce_scatter | solution.py:100
  140.7 44.4 %reduce-scatter.7.cloned.1.call-done = f32[80,2880]{1,0:T(8,128)} async-done(((f32[320,2880]{1,0:T(8,128)}), f32[80,2880]{1,0:T(8,128)}) %reduce-scatter.7.cloned.1.call-update) | async-done | bytes 921616
  188.3 3.4 collective-permute-start.6
  193.8 5.3 %collective-permute-done.7 = bf16[1,320,1,128]{3,1,2,0:T(8,128)(2,1)S(1)} collective-permute-done((bf16[1,320,1,128]{3,1,2,0:T(8,128)(2,1)S(1)}, bf16[1,320,1,128]{3,1,2,0:T(8,128)(2,1)S(1)}, u32[]{:S(2)}, u32[]{:S(2)}) %collective-permute-start.7) | collective-permute-done | bytes 81952 | tf_op jit(solution)/shard_map/ppermute | solution.py:18
  203.1 3.0 fusion.105
  206.5 10.6 %all-reduce.4 = (f32[1,32]{1,0:T(1,128)S(1)}, f32[1,32]{1,0:T(1,128)S(1)}, f32[1,320]{1,0:T(1,128)}) all-reduce(f32[1,32]{1,0:T(1,128)S(1)} %bitcast.372, f32[1,32]{1,0:T(1,128)S(1)} %bitcast.371, f32[1,320]{1,0:T(1,128)S(1)} %reduce_sum.242), channel_id=1, replica_groups=mesh['groups'=2,'rows'=4,'zero'=4] {'rows'}, use_global_device_ids=true, to_apply=%region_23.24 | all-reduce | flops 384 | bytes 3072 | tf_op jit(solution)/shard_map/psum | solution.py:61
  219.4 4.9 %fusion.59 = bf16[1,320,8,128]{3,1,2,0:T(8,128)(2,1)S(1)} fusion(bf16[1,9,320,8,128]{4,2,3,1,0:T(8,128)(2,1)} %copy-done.4, bf16[320,9,320]{2,0,1:T(8,128)(2,1)S(1)} %copy-done.7, bf16[1,320,8,128]{3,2,1,0:T(8,128)(2,1)S(1)} %copy-done), kind=kOutput, calls=%fused_computation.44 | convolution fusion | flops 1888419840 | bytes 9052160 | tf_op jit(solution)/shard_map/otc,ntchw->nohw/dot_general | solution.py:82
  225.6 32.3 %psum.79 = f32[4,320]{1,0:T(4,128)} all-reduce(f32[4,320]{1,0:T(4,128)S(1)} %pad_maximum_fusion.8), channel_id=1, replica_groups=mesh['groups'=2,'rows'=4,'zero'=4] {'rows','zero'}, use_global_device_ids=true, to_apply=%region_34.35 | all-reduce | flops 1280 | bytes 10240 | tf_op jit(solution)/shard_map/psum | solution.py:147
  257.9 14.0 %all-gather.11.cloned.1.call-done = f32[320,9,320]{2,0,1:T(8,128)} async-done(((f32[80,9,320]{2,0,1:T(8,128)}), f32[320,9,320]{2,0,1:T(8,128)}) %all-gather.11.cloned.1.call-update) | async-done | bytes 3686416 | tf_op jit(solution)/shard_map/all_gather | solution.py:106
  271.9 3.6 reduce_sum.243
  275.5 81.6 %all-gather.13.cloned.1.call-done = f32[320,9,320]{2,0,1:T(8,128)} async-done(((f32[80,9,320]{2,0,1:T(8,128)}), f32[320,9,320]{2,0,1:T(8,128)}) %all-gather.13.cloned.1.call-update) | async-done | bytes 3686416 | tf_op jit(solution)/shard_map/all_gather | solution.py:106
  357.1 3.6 reduce_sum.244
  (139 shorter events, 45.7 us)
Async XLA Ops:
  7.2 17.3 %copy-start = (bf16[1,320,8,128]{3,2,1,0:T(8,128)(2,1)S(1)}, bf16[1,320,8,128]{3,2,1,0:T(8,128)(2,1)}, u32[]{:S(2)}) copy-start(bf16[1,320,8,128]{3,2,1,0:T(8,128)(2,1)} %param.7) | copy-start | bytes 1966084
  7.2 20.5 %copy-start.1 = (bf16[1,320,8,128]{3,2,1,0:T(8,128)(2,1)S(1)}, bf16[1,320,8,128]{3,2,1,0:T(8,128)(2,1)}, u32[]{:S(2)}) copy-start(bf16[1,320,8,128]{3,2,1,0:T(8,128)(2,1)} %param.13) | copy-start | bytes 1966084
  7.2 44.6 %all-gather.7.cloned.1.call-start = ((), (), s32[]{:S(2)}) async-start(), calls=%async_computation.2 | async-start | bytes 2764800 | tf_op jit(solution)/shard_map/all_gather | solution.py:84
  7.9 60.1 %all-gather.9.cloned.1.call-start = ((), (), s32[]{:S(2)}) async-start(), calls=%async_computation.3 | async-start | bytes 2764800 | tf_op jit(solution)/shard_map/all_gather | solution.py:84
  24.4 9.3 %copy-start.5 = (f32[1,320]{1,0:T(1,128)S(1)}, f32[1,320]{1,0:T(1,128)}, u32[]{:S(2)}) copy-start(f32[1,320]{1,0:T(1,128)} %param.8) | copy-start | bytes 3844
  25.1 8.7 %collective-permute-start = (bf16[1,320,1,128]{3,1,2,0:T(8,128)(2,1)S(1)}, bf16[1,320,1,128]{3,1,2,0:T(8,128)(2,1)S(1)}, u32[]{:S(2)}, u32[]{:S(2)}) collective-permute-start(bf16[1,320,1,128]{3,1,2,0:T(8,128)(2,1)S(1)} %get-tuple-element.58), channel_id=1, source_target_pairs={{0,4},{4,8},{8,12},{1,5},{5,9},{9,13},{2,6},{6,10},{10,14},{3,7},{... | collective-permute-start | bytes 245768 | tf_op jit(solution)/shard_map/ppermute | solution.py:17
  26.4 7.4 %collective-permute-start.1 = (bf16[1,320,1,128]{3,1,2,0:T(8,128)(2,1)S(1)}, bf16[1,320,1,128]{3,1,2,0:T(8,128)(2,1)S(1)}, u32[]{:S(2)}, u32[]{:S(2)}) collective-permute-start(bf16[1,320,1,128]{3,1,2,0:T(8,128)(2,1)S(1)} %get-tuple-element.59), channel_id=1, source_target_pairs={{4,0},{8,4},{12,8},{5,1},{9,5},{13,9},{6,2},{10,6},{14,10},{7,3},{... | collective-permute-start | bytes 245768 | tf_op jit(solution)/shard_map/ppermute | solution.py:18
  27.8 8.9 %collective-permute-start.4 = (bf16[1,320,1,128]{3,1,2,0:T(8,128)(2,1)S(1)}, bf16[1,320,1,128]{3,1,2,0:T(8,128)(2,1)S(1)}, u32[]{:S(2)}, u32[]{:S(2)}) collective-permute-start(bf16[1,320,1,128]{3,1,2,0:T(8,128)(2,1)S(1)} %get-tuple-element.54), channel_id=1, source_target_pairs={{0,4},{4,8},{8,12},{1,5},{5,9},{9,13},{2,6},{6,10},{10,14},{3,7},{... | collective-permute-start | bytes 245768 | tf_op jit(solution)/shard_map/ppermute | solution.py:17
  32.4 6.3 %collective-permute-start.5 = (bf16[1,320,1,128]{3,1,2,0:T(8,128)(2,1)S(1)}, bf16[1,320,1,128]{3,1,2,0:T(8,128)(2,1)S(1)}, u32[]{:S(2)}, u32[]{:S(2)}) collective-permute-start(bf16[1,320,1,128]{3,1,2,0:T(8,128)(2,1)S(1)} %get-tuple-element.55), channel_id=1, source_target_pairs={{4,0},{8,4},{12,8},{5,1},{9,5},{13,9},{6,2},{10,6},{14,10},{7,3},{... | collective-permute-start | bytes 245768 | tf_op jit(solution)/shard_map/ppermute | solution.py:18
  33.7 106.9 %reduce-scatter.5.cloned.1.call-start = ((), (), s32[]{:S(2)}) async-start(), calls=%async_computation.4 | async-start | bytes 5529600 | tf_op jit(solution)/shard_map/reduce_scatter | solution.py:100
  48.3 2.5 copy-start.3
  95.8 89.3 %reduce-scatter.7.cloned.1.call-start = ((), (), s32[]{:S(2)}) async-start(), calls=%async_computation.7 | async-start | bytes 4710400
  95.9 4.9 %collective-permute-start.2 = (bf16[1,320,1,128]{3,1,2,0:T(8,128)(2,1)S(1)}, bf16[1,320,1,128]{3,1,2,0:T(8,128)(2,1)S(1)}, u32[]{:S(2)}, u32[]{:S(2)}) collective-permute-start(bf16[1,320,1,128]{3,1,2,0:T(8,128)(2,1)S(1)} %get-tuple-element.56), channel_id=1, source_target_pairs={{0,4},{4,8},{8,12},{1,5},{5,9},{9,13},{2,6},{6,10},{10,14},{3,7},{... | collective-permute-start | bytes 245768 | tf_op jit(solution)/shard_map/ppermute | solution.py:17
  98.8 6.3 %collective-permute-start.3 = (bf16[1,320,1,128]{3,1,2,0:T(8,128)(2,1)S(1)}, bf16[1,320,1,128]{3,1,2,0:T(8,128)(2,1)S(1)}, u32[]{:S(2)}, u32[]{:S(2)}) collective-permute-start(bf16[1,320,1,128]{3,1,2,0:T(8,128)(2,1)S(1)} %get-tuple-element.57), channel_id=1, source_target_pairs={{4,0},{8,4},{12,8},{5,1},{9,5},{13,9},{6,2},{10,6},{14,10},{7,3},{... | collective-permute-start | bytes 245768 | tf_op jit(solution)/shard_map/ppermute | solution.py:18
  107.9 4.9 %copy-start.4 = (bf16[1,9,320,8,128]{4,2,3,1,0:T(8,128)(2,1)}, bf16[1,9,320,8,128]{4,2,3,1,0:T(8,128)(2,1)S(1)}, u32[]{:S(2)}) copy-start(bf16[1,9,320,8,128]{4,2,3,1,0:T(8,128)(2,1)S(1)} %fusion.131) | copy-start | bytes 17694724
  118.8 153.0 %all-gather.11.cloned.1.call-start = ((), (), s32[]{:S(2)}) async-start(), calls=%async_computation.5 | async-start | bytes 5529600 | tf_op jit(solution)/shard_map/all_gather | solution.py:106
  140.7 216.4 %all-gather.13.cloned.1.call-start = ((), (), s32[]{:S(2)}) async-start(), calls=%async_computation.6 | async-start | bytes 5529600 | tf_op jit(solution)/shard_map/all_gather | solution.py:106
  188.3 5.4 %collective-permute-start.6 = (bf16[1,320,1,128]{3,1,2,0:T(8,128)(2,1)S(1)}, bf16[1,320,1,128]{3,1,2,0:T(8,128)(2,1)S(1)}, u32[]{:S(2)}, u32[]{:S(2)}) collective-permute-start(bf16[1,320,1,128]{3,1,2,0:T(8,128)(2,1)S(1)} %get-tuple-element.52), channel_id=1, source_target_pairs={{0,4},{4,8},{8,12},{1,5},{5,9},{9,13},{2,6},{6,10},{10,14},{3,7},{... | collective-permute-start | bytes 245768 | tf_op jit(solution)/shard_map/ppermute | solution.py:17
  191.7 7.3 %collective-permute-start.7 = (bf16[1,320,1,128]{3,1,2,0:T(8,128)(2,1)S(1)}, bf16[1,320,1,128]{3,1,2,0:T(8,128)(2,1)S(1)}, u32[]{:S(2)}, u32[]{:S(2)}) collective-permute-start(bf16[1,320,1,128]{3,1,2,0:T(8,128)(2,1)S(1)} %get-tuple-element.53), channel_id=1, source_target_pairs={{4,0},{8,4},{12,8},{5,1},{9,5},{13,9},{6,2},{10,6},{14,10},{7,3},{... | collective-permute-start | bytes 245768 | tf_op jit(solution)/shard_map/ppermute | solution.py:18
  201.4 1.6 copy-start.6
  203.0 14.4 %copy-start.2 = (bf16[1,320,8,128]{3,2,1,0:T(8,128)(2,1)S(1)}, bf16[1,320,8,128]{3,2,1,0:T(8,128)(2,1)}, u32[]{:S(2)}) copy-start(bf16[1,320,8,128]{3,2,1,0:T(8,128)(2,1)} %param.13) | copy-start | bytes 1966084
  217.5 1.9 copy-start.7
Sparse Core Ops, SparseCore 0:
  9.6 25.9 all-gather.6
  37.1 23.2 all-gather.8
  96.0 44.6 reduce-scatter.4
  143.2 41.8 reduce-scatter.6
  186.5 85.3 all-gather.10
  273.9 83.1 all-gather.12
